TPU v7x, 32 devices: a whole 2x2x4 slice. The times are simulated.
32 devices in a mesh: dp: 8 (over y, x, core), tensor: 4 (over z).
Axes of the slice: x: 2, y: 2, z: 4, core: 2. Of those that a mesh axis runs over, the one named last changes fastest.
Arguments:
- hidden_in: bfloat16 [8192, 768], P(('dp', 'tensor')), may hold values from -40 to 40
- segment_ids: int32 [16, 512], P('dp'), may hold values from 0 to 7, never falling along the last dimension, each value on 1 to 256 neighbouring positions
- cotangent: float32 [8192, 768], P(('dp', 'tensor')), may hold values from -6 to 6
- norm1_gain: float32 [768], P(('dp', 'tensor')), may hold values from 0.5 to 1.5
- norm1_bias: float32 [768], P(('dp', 'tensor')), may hold values from -2 to 2
- norm2_gain: float32 [768], P(('dp', 'tensor')), may hold values from 0.5 to 1.5
- norm2_bias: float32 [768], P(('dp', 'tensor')), may hold values from -2 to 2
- qkv_weight: bfloat16 [768, 2304], P('dp', 'tensor'), may hold values from -2 to 2
- qkv_bias: bfloat16 [12, 192], P('tensor', 'dp'), may hold values from -3 to 3
- dense_weight: bfloat16 [768, 768], P('tensor', 'dp'), may hold values from -0.875 to 0.875
- dense_bias: float32 [768], P(('dp', 'tensor')), may hold values from -3 to 3
- up_weight: bfloat16 [768, 3072], P('dp', 'tensor'), may hold values from -0.21875 to 0.21875
- up_bias: bfloat16 [12, 256], P('tensor', 'dp'), may hold values from -3 to 3
- down_weight: bfloat16 [3072, 768], P('tensor', 'dp'), may hold values from -0.109375 to 0.109375
- down_bias: float32 [768], P(('dp', 'tensor')), may hold values from -3 to 3
Outputs:
- hidden_out: float32 [8192, 768], P(('dp', 'tensor'))
- hidden_grad: float32 [8192, 768], P(('dp', 'tensor'))
- norm1_gain_grad: float32 [768], P(('dp', 'tensor'))
- norm1_bias_grad: float32 [768], P(('dp', 'tensor'))
- norm2_gain_grad: float32 [768], P(('dp', 'tensor'))
- norm2_bias_grad: float32 [768], P(('dp', 'tensor'))
- qkv_weight_grad: float32 [768, 2304], P('dp', 'tensor')
- qkv_bias_grad: float32 [12, 192], P('tensor', 'dp')
- dense_weight_grad: float32 [768, 768], P('tensor', 'dp')
- dense_bias_grad: float32 [768], P(('dp', 'tensor'))
- up_weight_grad: float32 [768, 3072], P('dp', 'tensor')
- up_bias_grad: float32 [12, 256], P('tensor', 'dp')
- down_weight_grad: float32 [3072, 768], P('tensor', 'dp')
- down_bias_grad: float32 [768], P(('dp', 'tensor'))
Inputs may be any that keep to these rules, and one draw needn't show every extreme that they name: `segment_ids`: within each row of 512 tokens the ids never fall; each document holds 1 to 256 tokens, and some document holds exactly 256.
All inputs are finite; a program needn't handle non-finite values.
Results may differ from a plain program's by a relative error of at most 0.0082.
Values may be sent and summed in bfloat16 or wider, within the bound.
No kernel may reach another device: no remote copies, remote signals or barrier semaphores. Data moves between devices by JAX's collectives and lax.ppermute only.
A program may use at most 128 MiB of HBM per device.

v0:
```python
import math
import jax
import jax.numpy as jnp
from jax import lax
from jax.sharding import PartitionSpec as P

HD = 64
ROT = 16
BIAS_ROW = 256
norm_eps = 1e-05


def rotary_tables(length, rot_dims):
    places = jnp.arange(length).astype(jnp.float32)
    frequency = 1.0 / 10000.0 ** (jnp.arange(0, rot_dims, 2).astype(jnp.float32) / rot_dims)
    angles = places[:, None] * frequency[None, :]
    angles = jnp.concatenate([angles, angles], axis=1)
    return (jnp.cos(angles)[:, None, :], jnp.sin(angles)[:, None, :])


def rotate_apply(entries, cosine, sine, rot_dims):
    half_dims = rot_dims // 2
    front = entries[..., :rot_dims]
    turned = jnp.concatenate([-front[..., half_dims:], front[..., :half_dims]], axis=-1)
    return jnp.concatenate([front * cosine + turned * sine, entries[..., rot_dims:]], axis=-1)


def rotate_back(grads, cosine, sine, rot_dims):
    half_dims = rot_dims // 2
    front = grads[..., :rot_dims]
    scaled = front * sine
    turned = jnp.concatenate([scaled[..., half_dims:], -scaled[..., :half_dims]], axis=-1)
    return jnp.concatenate([front * cosine + turned, grads[..., rot_dims:]], axis=-1)


def normalize(wide_rows):
    centre = jnp.mean(wide_rows, axis=-1, keepdims=True)
    spread = jnp.mean(jnp.square(wide_rows - centre), axis=-1, keepdims=True)
    inverse = lax.rsqrt(spread + norm_eps)
    return ((wide_rows - centre) * inverse, inverse)


def gelu_exact(values):
    return 0.5 * values * (1.0 + lax.erf(values * (1.0 / math.sqrt(2.0))))


def gelu_slope(values):
    cumulative = 0.5 * (1.0 + lax.erf(values * (1.0 / math.sqrt(2.0))))
    density = jnp.exp(-0.5 * values * values) * (1.0 / math.sqrt(2.0 * math.pi))
    return cumulative + values * density


def allowed_pairs(segment):
    length = segment.shape[-1]
    earlier = lax.broadcasted_iota(jnp.int32, (length, length), 0) >= lax.broadcasted_iota(
        jnp.int32, (length, length), 1
    )
    return (segment[:, :, None] == segment[:, None, :]) & earlier[None]


def attend_scores(queries, key_rows, segment):
    scaling = queries.shape[-1] ** (-0.5)
    scores = (
        jnp.einsum("bqhd,bkhd->bhqk", queries, key_rows, preferred_element_type=jnp.float32)
        * scaling
    )
    return jnp.where(allowed_pairs(segment)[:, None], scores, -1e30)


def attend_forward(queries, key_rows, value_rows, segment):
    scores = attend_scores(queries, key_rows, segment)
    highest = jnp.max(scores, axis=-1, keepdims=True)
    logsum = highest + jnp.log(jnp.sum(jnp.exp(scores - highest), axis=-1, keepdims=True))
    weights = jnp.exp(scores - logsum).astype(jnp.bfloat16)
    output = jnp.einsum("bhqk,bkhd->bqhd", weights, value_rows, preferred_element_type=jnp.float32)
    return (output.astype(jnp.bfloat16), logsum)


def attend_backward(queries, key_rows, value_rows, segment, logsum, grad_out):
    scaling = queries.shape[-1] ** (-0.5)
    scores = attend_scores(queries, key_rows, segment)
    weights = jnp.exp(scores - logsum)
    weights_half = weights.astype(jnp.bfloat16)
    grad_weights = jnp.einsum(
        "bqhd,bkhd->bhqk", grad_out, value_rows, preferred_element_type=jnp.float32
    )
    inner_sum = jnp.sum(weights * grad_weights, axis=-1, keepdims=True)
    grad_scores = (weights * (grad_weights - inner_sum) * scaling).astype(jnp.bfloat16)
    grad_queries = jnp.einsum(
        "bhqk,bkhd->bqhd", grad_scores, key_rows, preferred_element_type=jnp.float32
    )
    grad_keys = jnp.einsum(
        "bhqk,bqhd->bkhd", grad_scores, queries, preferred_element_type=jnp.float32
    )
    grad_values = jnp.einsum(
        "bhqk,bqhd->bkhd", weights_half, grad_out, preferred_element_type=jnp.float32
    )
    return (grad_queries, grad_keys, grad_values)


def rows_product(left, right):
    return lax.dot_general(
        left, right, (((0,), (0,)), ((), ())), preferred_element_type=jnp.float32
    )


def cols_product(left, right):
    return lax.dot_general(
        left, right, (((1,), (1,)), ((), ())), preferred_element_type=jnp.float32
    )


def on_device(
    hidden_in,
    segment_ids,
    cotangent,
    norm1_gain,
    norm1_bias,
    norm2_gain,
    norm2_bias,
    qkv_weight,
    qkv_bias,
    dense_weight,
    dense_bias,
    up_weight,
    up_bias,
    down_weight,
    down_bias,
):
    gain_one, shift_one, gain_two, shift_two, dense_shift, down_shift = (
        lax.all_gather(norm1_gain, ("dp", "tensor"), axis=0, tiled=True),
        lax.all_gather(norm1_bias, ("dp", "tensor"), axis=0, tiled=True),
        lax.all_gather(norm2_gain, ("dp", "tensor"), axis=0, tiled=True),
        lax.all_gather(norm2_bias, ("dp", "tensor"), axis=0, tiled=True),
        lax.all_gather(dense_bias, ("dp", "tensor"), axis=0, tiled=True),
        lax.all_gather(down_bias, ("dp", "tensor"), axis=0, tiled=True),
    )
    qkv_full, up_full = (
        lax.all_gather(qkv_weight, "dp", axis=0, tiled=True),
        lax.all_gather(up_weight, "dp", axis=0, tiled=True),
    )
    dense_full, down_full, qkv_shift, up_shift = (
        lax.all_gather(dense_weight, "dp", axis=1, tiled=True),
        lax.all_gather(down_weight, "dp", axis=1, tiled=True),
        lax.all_gather(qkv_bias, "dp", axis=1, tiled=True),
        lax.all_gather(up_bias, "dp", axis=1, tiled=True),
    )
    seq_count = segment_ids.shape[0]
    length = segment_ids.shape[1]
    heads_here = qkv_full.shape[1] // (3 * HD)
    cosine, sine = rotary_tables(length, ROT)
    wide_rows = hidden_in.astype(jnp.float32)
    normed, inverse = normalize(wide_rows)
    first_local = (normed * gain_one + shift_one).astype(jnp.bfloat16)
    second_local = (normed * gain_two + shift_two).astype(jnp.bfloat16)
    first, second = (
        lax.all_gather(first_local, "tensor", axis=0, tiled=True),
        lax.all_gather(second_local, "tensor", axis=0, tiled=True),
    )
    mixed = jnp.dot(first, qkv_full, preferred_element_type=jnp.float32) + qkv_shift.reshape(
        -1
    ).astype(jnp.float32)
    mixed = mixed.reshape(seq_count, length, heads_here, 3, HD)
    queries = rotate_apply(mixed[..., 0, :], cosine, sine, ROT).astype(jnp.bfloat16)
    key_rows = rotate_apply(mixed[..., 1, :], cosine, sine, ROT).astype(jnp.bfloat16)
    value_rows = mixed[..., 2, :].astype(jnp.bfloat16)
    attended, logsum = attend_forward(queries, key_rows, value_rows, segment_ids)
    attended_flat = attended.reshape(seq_count * length, heads_here * HD)
    inner_pre = jnp.dot(second, up_full, preferred_element_type=jnp.float32) + up_shift.reshape(
        -1
    ).astype(jnp.float32)
    active = gelu_exact(inner_pre).astype(jnp.bfloat16)
    partial_value = jnp.dot(
        attended_flat, dense_full, preferred_element_type=jnp.float32
    ) + jnp.dot(active, down_full, preferred_element_type=jnp.float32)
    branch = lax.psum_scatter(partial_value, "tensor", scatter_dimension=0, tiled=True)
    hidden_out = wide_rows + branch + dense_shift + down_shift
    qkv_back, up_back = (
        lax.all_gather(qkv_weight, "dp", axis=0, tiled=True),
        lax.all_gather(up_weight, "dp", axis=0, tiled=True),
    )
    dense_back, down_back = (
        lax.all_gather(dense_weight, "dp", axis=1, tiled=True),
        lax.all_gather(down_weight, "dp", axis=1, tiled=True),
    )
    cotangent_all = lax.all_gather(cotangent.astype(jnp.bfloat16), "tensor", axis=0, tiled=True)
    grad_down = rows_product(active, cotangent_all)
    grad_active = cols_product(cotangent_all, down_back)
    grad_pre = grad_active * gelu_slope(inner_pre)
    grad_pre_half = grad_pre.astype(jnp.bfloat16)
    grad_up = rows_product(second, grad_pre_half)
    second_part = cols_product(grad_pre_half, up_back)
    grad_dense = rows_product(attended_flat, cotangent_all)
    grad_attended = (
        cols_product(cotangent_all, dense_back)
        .astype(jnp.bfloat16)
        .reshape(seq_count, length, heads_here, HD)
    )
    grad_queries, grad_keys, grad_values = attend_backward(
        queries, key_rows, value_rows, segment_ids, logsum, grad_attended
    )
    grad_mixed = jnp.stack(
        [
            rotate_back(grad_queries, cosine, sine, ROT),
            rotate_back(grad_keys, cosine, sine, ROT),
            grad_values,
        ],
        axis=3,
    )
    grad_mixed = grad_mixed.reshape(seq_count * length, heads_here * 3 * HD)
    grad_mixed_half = grad_mixed.astype(jnp.bfloat16)
    grad_qkv = rows_product(first, grad_mixed_half)
    first_part = cols_product(grad_mixed_half, qkv_back)
    grad_first, grad_second = (
        lax.psum_scatter(first_part, "tensor", scatter_dimension=0, tiled=True),
        lax.psum_scatter(second_part, "tensor", scatter_dimension=0, tiled=True),
    )
    grad_normed = grad_first * gain_one + grad_second * gain_two
    stat_terms = (
        jnp.sum(grad_first * normed, axis=0),
        jnp.sum(grad_first, axis=0),
        jnp.sum(grad_second * normed, axis=0),
        jnp.sum(grad_second, axis=0),
    )
    grad_rows = inverse * (
        grad_normed
        - jnp.mean(grad_normed, axis=-1, keepdims=True)
        - normed * jnp.mean(grad_normed * normed, axis=-1, keepdims=True)
    )
    hidden_grad = cotangent + grad_rows
    gain_one_grad, shift_one_grad, gain_two_grad, shift_two_grad, shift_out_grad = (
        lax.psum_scatter(stat_terms[0], ("dp", "tensor"), scatter_dimension=0, tiled=True),
        lax.psum_scatter(stat_terms[1], ("dp", "tensor"), scatter_dimension=0, tiled=True),
        lax.psum_scatter(stat_terms[2], ("dp", "tensor"), scatter_dimension=0, tiled=True),
        lax.psum_scatter(stat_terms[3], ("dp", "tensor"), scatter_dimension=0, tiled=True),
        lax.psum_scatter(
            jnp.sum(cotangent, axis=0), ("dp", "tensor"), scatter_dimension=0, tiled=True
        ),
    )
    qkv_grad, up_grad = (
        lax.psum_scatter(grad_qkv, "dp", scatter_dimension=0, tiled=True),
        lax.psum_scatter(grad_up, "dp", scatter_dimension=0, tiled=True),
    )
    dense_grad, down_grad, qkv_bias_grad, up_bias_grad = (
        lax.psum_scatter(grad_dense, "dp", scatter_dimension=1, tiled=True),
        lax.psum_scatter(grad_down, "dp", scatter_dimension=1, tiled=True),
        lax.psum_scatter(
            jnp.sum(grad_mixed, axis=0).reshape(heads_here, 3 * HD),
            "dp",
            scatter_dimension=1,
            tiled=True,
        ),
        lax.psum_scatter(
            jnp.sum(grad_pre, axis=0).reshape(-1, BIAS_ROW), "dp", scatter_dimension=1, tiled=True
        ),
    )
    return (
        hidden_out,
        hidden_grad,
        gain_one_grad,
        shift_one_grad,
        gain_two_grad,
        shift_two_grad,
        qkv_grad,
        qkv_bias_grad,
        dense_grad,
        shift_out_grad,
        up_grad,
        up_bias_grad,
        down_grad,
        shift_out_grad,
    )


def solution(mesh):
    return jax.shard_map(
        on_device,
        mesh=mesh,
        in_specs=(
            P(("dp", "tensor"), None),
            P("dp", None),
            P(("dp", "tensor"), None),
            P(("dp", "tensor")),
            P(("dp", "tensor")),
            P(("dp", "tensor")),
            P(("dp", "tensor")),
            P("dp", "tensor"),
            P("tensor", "dp"),
            P("tensor", "dp"),
            P(("dp", "tensor")),
            P("dp", "tensor"),
            P("tensor", "dp"),
            P("tensor", "dp"),
            P(("dp", "tensor")),
        ),
        out_specs=(
            P(("dp", "tensor"), None),
            P(("dp", "tensor"), None),
            P(("dp", "tensor")),
            P(("dp", "tensor")),
            P(("dp", "tensor")),
            P(("dp", "tensor")),
            P("dp", "tensor"),
            P("tensor", "dp"),
            P("tensor", "dp"),
            P(("dp", "tensor")),
            P("dp", "tensor"),
            P("tensor", "dp"),
            P("tensor", "dp"),
            P(("dp", "tensor")),
        ),
        check_vma=False,
    )
```

profile of v0, /device:TPU:0, one launch (start us, length us, event | category | flops | bytes accessed | tf_op | source)
XLA Modules:
  0.0 633.8 jit_solution(11862884323727938177)
XLA Ops:
  13.1 42.2 %all-reduce.13 = (f32[768]{0:T(1024)S(1)}, f32[768]{0:T(1024)S(1)}, f32[768]{0:T(1024)S(1)}, f32[768]{0:T(1024)S(1)}) all-reduce(f32[768]{0:T(1024)S(1)} %dynamic-update-slice.3, f32[768]{0:T(1024)S(1)} %dynamic-update-slice.2, f32[768]{0:T(1024)S(1)} %dynamic-update-slice.1, ...), channel_id=1, replica_groups=mesh['dp'=8,'tensor'=4] {'dp','tensor'}, use_global_device_ids=true, to_apply=%add.3 | all-reduce | flops 3072 | bytes 24576
  61.6 11.6 %all_gather.52 = bf16[768,576]{1,0:T(8,128)(2,1)S(1)} all-gather(bf16[96,576]{1,0:T(8,128)(2,1)S(1)} %copy-done.18), channel_id=1, replica_groups=mesh['dp'=8,'tensor'=4] {'dp'}, dimensions={0}, use_global_device_ids=true | all-gather | bytes 995328 | tf_op jit(solution)/shard_map/all_gather | solution.py:139
  73.2 7.9 %all-gather = bf16[8,24,3]{1,2,0:T(4,128)(2,1)S(1)} all-gather(bf16[1,24,3]{1,2,0:T(4,128)(2,1)S(1)} %bitcast.91), channel_id=1, replica_groups=mesh['dp'=8,'tensor'=4] {'dp'}, dimensions={0}, use_global_device_ids=true | all-gather | bytes 1296 | tf_op jit(solution)/shard_map/all_gather | solution.py:145
  81.5 9.6 %all_gather.54 = bf16[192,768]{0,1:T(8,128)(2,1)S(1)} all-gather(bf16[192,96]{0,1:T(8,128)(2,1)S(1)} %copy.86), channel_id=1, replica_groups=mesh['dp'=8,'tensor'=4] {'dp'}, dimensions={1}, use_global_device_ids=true | all-gather | bytes 331776 | tf_op jit(solution)/shard_map/all_gather | solution.py:143
  91.1 7.9 %all-gather.1 = bf16[8,32,3]{1,2,0:T(4,128)(2,1)S(1)} all-gather(bf16[1,32,3]{1,2,0:T(4,128)(2,1)S(1)} %bitcast.92), channel_id=1, replica_groups=mesh['dp'=8,'tensor'=4] {'dp'}, dimensions={0}, use_global_device_ids=true | all-gather | bytes 1728 | tf_op jit(solution)/shard_map/all_gather | solution.py:146
  100.2 4.1 convolution_add_fusion.1
  104.4 3.8 reshape.175
  114.3 18.3 %all-gather.16.cloned.1.call-done = bf16[1024,768]{1,0:T(8,128)(2,1)} async-done(((bf16[256,768]{1,0:T(8,128)(2,1)}), bf16[1024,768]{1,0:T(8,128)(2,1)}) %all-gather.16.cloned.1.call-update) | async-done | bytes 1572880 | tf_op jit(solution)/shard_map/all_gather | solution.py:186
  135.0 3.7 fusion.66
  138.7 12.8 %fusion.27 = f32[2,512,3,64]{1,3,2,0:T(8,128)S(1)} fusion(f32[2,3,512,512]{2,3,1,0:T(8,128)} %fusion.66, bf16[2,512,3,48]{1,3,2,0:T(8,128)(2,1)S(1)} %copy-done.16, bf16[2,512,3,16]{1,3,2,0:T(8,128)(2,1)S(1)} %get-tuple-element.51, f32[2,3,512,512]{2,3,1,0:T(8,128)} %copy-done.1, f32[2,3,512]{2,1,0:T(4,128)S(1)} %log_add_fusion, ...), kind=kOutput, calls=%fused_computation.31 | convolution fusion | flops 219418112 | bytes 14299136 | tf_op jit(solution)/shard_map/bhqk,bkhd->bqhd/dot_general | solution.py:89
  152.4 13.1 %fusion.30 = f32[2,512,3,64]{1,3,2,0:T(8,128)S(1)} fusion(f32[2,3,512,512]{2,3,1,0:T(8,128)} %fusion.66, bf16[2,512,3,48]{1,3,2,0:T(8,128)(2,1)} %copy-done.17, bf16[2,512,3,16]{1,3,2,0:T(8,128)(2,1)S(1)} %get-tuple-element.50, f32[2,3,512,512]{2,3,1,0:T(8,128)} %copy-done.1, f32[2,3,512]{2,1,0:T(4,128)S(1)} %log_add_fusion, ...), kind=kOutput, calls=%fused_computation.32 | convolution fusion | flops 219418112 | bytes 14299136 | tf_op jit(solution)/shard_map/bhqk,bqhd->bkhd/dot_general | solution.py:92
  166.4 4.6 fusion.36
  171.7 24.1 %all-gather.10.cloned.1.call-done = bf16[1024,768]{1,0:T(8,128)(2,1)} async-done(((bf16[256,768]{1,0:T(8,128)(2,1)}), bf16[1024,768]{1,0:T(8,128)(2,1)}) %all-gather.10.cloned.1.call-update) | async-done | bytes 1572880 | tf_op jit(solution)/shard_map/all_gather | solution.py:158
  195.7 5.4 multiply_convert_fusion.1
  201.2 19.1 %all-gather.14.cloned.1.call-done = bf16[768,768]{0,1:T(8,128)(2,1)} async-done(((bf16[768,96]{0,1:T(8,128)(2,1)}), bf16[768,768]{0,1:T(8,128)(2,1)}) %all-gather.14.cloned.1.call-update) | async-done | bytes 1179664 | tf_op jit(solution)/shard_map/all_gather | solution.py:144
  220.3 5.6 fusion.90
  234.4 4.8 fusion.24
  242.0 3.2 fusion.92
  245.3 4.8 fusion.62
  250.4 3.2 fusion.91
  256.0 4.5 fusion.93
  260.6 4.8 fusion.60
  265.4 4.3 fusion.94
  274.9 13.1 %all-reduce.10 = f32[3,192]{1,0:T(4,128)S(1)} all-reduce(f32[3,192]{1,0:T(4,128)S(1)} %reshape.178), channel_id=10, replica_groups=mesh['dp'=8,'tensor'=4] {'dp'}, use_global_device_ids=true, to_apply=%region_20.21.clone | all-reduce | flops 576 | bytes 4608
  289.9 11.2 %reduce-scatter.26.cloned.1.call-done = f32[96,192]{1,0:T(8,128)} async-done(((f32[768,192]{1,0:T(8,128)}), f32[96,192]{1,0:T(8,128)}) %reduce-scatter.26.cloned.1.call-update) | async-done | bytes 73744
  302.8 61.1 %reduce-scatter.16.cloned.1.call-done = f32[256,768]{1,0:T(8,128)} async-done(((f32[1024,768]{1,0:T(8,128)}), f32[256,768]{1,0:T(8,128)}) %reduce-scatter.16.cloned.1.call-update) | async-done | bytes 786448 | tf_op jit(solution)/shard_map/reduce_scatter | solution.py:215
  363.9 62.7 %reduce-scatter.18.cloned.1.call-done = f32[256,768]{1,0:T(8,128)} async-done(((f32[1024,768]{1,0:T(8,128)}), f32[256,768]{1,0:T(8,128)}) %reduce-scatter.18.cloned.1.call-update) | async-done | bytes 786448 | tf_op jit(solution)/shard_map/reduce_scatter | solution.py:216
  429.6 43.5 %all-reduce.12 = (f32[768]{0:T(1024)S(1)}, f32[768]{0:T(1024)S(1)}, f32[768]{0:T(1024)S(1)}, f32[768]{0:T(1024)S(1)}, f32[768]{0:T(1024)S(1)}, /*index=5*/f32[768]{0:T(1024)S(1)}, f32[768]{0:T(1024)S(1)}) all-reduce(f32[768]{0:T(1024)S(1)} %dynamic-update-slice.5, ...), channel_id=1, replica_groups=mesh['dp'=8,'tensor'=4] {'dp','tensor'}, use_global_device_ids=true, to_apply=%add.5 | all-reduce | flops 5376 | bytes 43008
  475.5 14.4 %reduce-scatter.14.cloned.1.call-done = f32[256,768]{1,0:T(8,128)} async-done(((f32[1024,768]{1,0:T(8,128)}), f32[256,768]{1,0:T(8,128)}) %reduce-scatter.14.cloned.1.call-update) | async-done | bytes 786448 | tf_op jit(solution)/shard_map/reduce_scatter | solution.py:176
  492.0 42.1 %reduce-scatter.20.cloned.1.call-done = f32[96,576]{1,0:T(8,128)} async-done(((f32[768,576]{1,0:T(8,128)}), f32[96,576]{1,0:T(8,128)}) %reduce-scatter.20.cloned.1.call-update) | async-done | bytes 221200 | tf_op jit(solution)/shard_map/reduce_scatter | solution.py:241
  534.1 46.1 %reduce-scatter.22.cloned.1.call-done = f32[96,768]{1,0:T(8,128)} async-done(((f32[768,768]{1,0:T(8,128)}), f32[96,768]{1,0:T(8,128)}) %reduce-scatter.22.cloned.1.call-update) | async-done | bytes 294928 | tf_op jit(solution)/shard_map/reduce_scatter | solution.py:242
  580.3 46.3 %reduce-scatter.24.cloned.1.call-done = f32[768,96]{0,1:T(8,128)} async-done(((f32[768,768]{0,1:T(8,128)}), f32[768,96]{0,1:T(8,128)}) %reduce-scatter.24.cloned.1.call-update) | async-done | bytes 294928 | tf_op jit(solution)/shard_map/reduce_scatter | solution.py:246
  (158 shorter events, 54.6 us)
Async XLA Ops:
  7.2 54.4 %copy-start.18 = (bf16[96,576]{1,0:T(8,128)(2,1)S(1)}, bf16[96,576]{1,0:T(8,128)(2,1)}, u32[]{:S(2)}) copy-start(bf16[96,576]{1,0:T(8,128)(2,1)} %param.22) | copy-start | bytes 331780
  7.2 66.0 %copy-start.22 = (bf16[3,24]{1,0:T(4,128)(2,1)S(1)}, bf16[3,24]{1,0:T(4,128)(2,1)}, u32[]{:S(2)}) copy-start(bf16[3,24]{1,0:T(4,128)(2,1)} %param.23) | copy-start | bytes 436
  7.2 74.2 %copy-start.19 = (bf16[192,96]{1,0:T(8,128)(2,1)S(1)}, bf16[192,96]{1,0:T(8,128)(2,1)}, u32[]{:S(2)}) copy-start(bf16[192,96]{1,0:T(8,128)(2,1)} %param.24) | copy-start | bytes 110596
  7.2 93.0 %all-gather.8.cloned.1.call-start = ((), (), s32[]{:S(2)}) async-start(), calls=%async_computation.8 | async-start | bytes 1966080 | tf_op jit(solution)/shard_map/all_gather | solution.py:157
  8.4 82.7 %copy-start.23 = (bf16[3,32]{1,0:T(4,128)(2,1)S(1)}, bf16[3,32]{1,0:T(4,128)(2,1)}, u32[]{:S(2)}) copy-start(bf16[3,32]{1,0:T(4,128)(2,1)} %param.27) | copy-start | bytes 580
  8.4 91.3 %copy-start.20 = (s32[2,512]{1,0:T(2,128)S(1)}, s32[2,512]{1,0:T(2,128)}, u32[]{:S(2)}) copy-start(s32[2,512]{1,0:T(2,128)} %param.16) | copy-start | bytes 12292
  57.5 75.1 %all-gather.16.cloned.1.call-start = ((), (), s32[]{:S(2)}) async-start(), calls=%async_computation.13 | async-start | bytes 1966080 | tf_op jit(solution)/shard_map/all_gather | solution.py:186
  59.5 112.2 %all-gather.12.cloned.1.call-start = ((), (), s32[]{:S(2)}) async-start(), calls=%async_computation.10 | async-start | bytes 1327104 | tf_op jit(solution)/shard_map/all_gather | solution.py:140
  60.2 135.5 %all-gather.10.cloned.1.call-start = ((), (), s32[]{:S(2)}) async-start(), calls=%async_computation.9 | async-start | bytes 1966080 | tf_op jit(solution)/shard_map/all_gather | solution.py:158
  60.8 159.5 %all-gather.14.cloned.1.call-start = ((), (), s32[]{:S(2)}) async-start(), calls=%async_computation.11 | async-start | bytes 1327104 | tf_op jit(solution)/shard_map/all_gather | solution.py:144
  61.4 227.2 %reduce-scatter.28.cloned.1.call-start = ((), (), s32[]{:S(2)}) async-start(), calls=%async_computation.20 | async-start | bytes 147456
  73.2 27.1 %copy-start.12 = (bf16[768,576]{1,0:T(8,128)(2,1)}, bf16[768,576]{1,0:T(8,128)(2,1)S(1)}, u32[]{:S(2)}) copy-start(bf16[768,576]{1,0:T(8,128)(2,1)S(1)} %all_gather.52) | copy-start | bytes 2654212
  81.4 28.8 %copy-start.14 = (f32[512,16]{0,1:T(8,128)}, f32[512,16]{0,1:T(8,128)S(1)}, u32[]{:S(2)}) copy-start(f32[512,16]{0,1:T(8,128)S(1)} %get-tuple-element.56) | copy-start | bytes 98308
  100.2 66.2 %copy-start.7 = (pred[2,512,512]{1,2,0:T(8,128)(4,1)}, pred[2,512,512]{1,2,0:T(8,128)(4,1)S(1)}, u32[]{:S(2)}) copy-start(pred[2,512,512]{1,2,0:T(8,128)(4,1)S(1)} %compare_and_fusion) | copy-start | bytes 1572868
  114.3 20.7 %copy-start.9 = (bf16[2,512,3,1,64]{1,0,4,3,2:T(2,128)(2,1)S(1)}, bf16[2,512,3,1,64]{1,0,4,3,2:T(2,128)(2,1)}, u32[]{:S(2)}) copy-start(bf16[2,512,3,1,64]{1,0,4,3,2:T(2,128)(2,1)} %slice.83) | copy-start | bytes 1179652
  114.3 52.1 %copy-start.21 = (f32[2,3,512]{2,1,0:T(4,128)}, f32[2,3,512]{2,1,0:T(4,128)S(1)}, u32[]{:S(2)}) copy-start(f32[2,3,512]{2,1,0:T(4,128)S(1)} %log_add_fusion) | copy-start | bytes 36868
  134.9 3.7 copy-start.8
  134.9 3.7 copy-start.16
  165.5 6.0 copy-start.10
  171.5 60.0 %copy-start.3 = (bf16[24,8,2,512]{3,1,2,0:T(8,128)(2,1)}, bf16[24,8,2,512]{3,1,2,0:T(8,128)(2,1)S(1)}, u32[]{:S(2)}) copy-start(bf16[24,8,2,512]{3,1,2,0:T(8,128)(2,1)S(1)} %copy.108) | copy-start | bytes 1179652
  171.6 48.7 %copy-start.2 = (bf16[1024,768]{1,0:T(8,128)(2,1)S(1)}, bf16[1024,768]{1,0:T(8,128)(2,1)}, u32[]{:S(2)}) copy-start(bf16[1024,768]{1,0:T(8,128)(2,1)} %all-gather.16.cloned.1.call-done) | copy-start | bytes 4718596
  228.7 72.5 %reduce-scatter.26.cloned.1.call-start = ((), (), s32[]{:S(2)}) async-start(), calls=%async_computation.19 | async-start | bytes 884736
  234.3 129.5 %reduce-scatter.16.cloned.1.call-start = ((), (), s32[]{:S(2)}) async-start(), calls=%async_computation.14 | async-start | bytes 3932160 | tf_op jit(solution)/shard_map/reduce_scatter | solution.py:215
  245.3 181.3 %reduce-scatter.18.cloned.1.call-start = ((), (), s32[]{:S(2)}) async-start(), calls=%async_computation.15 | async-start | bytes 3932160 | tf_op jit(solution)/shard_map/reduce_scatter | solution.py:216
  250.1 239.8 %reduce-scatter.14.cloned.1.call-start = ((), (), s32[]{:S(2)}) async-start(), calls=%async_computation.12 | async-start | bytes 3932160 | tf_op jit(solution)/shard_map/reduce_scatter | solution.py:176
  250.4 3.2 copy-start.4
  256.0 278.2 %reduce-scatter.20.cloned.1.call-start = ((), (), s32[]{:S(2)}) async-start(), calls=%async_computation.16 | async-start | bytes 2211840 | tf_op jit(solution)/shard_map/reduce_scatter | solution.py:241
  260.5 319.7 %reduce-scatter.22.cloned.1.call-start = ((), (), s32[]{:S(2)}) async-start(), calls=%async_computation.17 | async-start | bytes 2654208 | tf_op jit(solution)/shard_map/reduce_scatter | solution.py:242
  265.4 361.2 %reduce-scatter.24.cloned.1.call-start = ((), (), s32[]{:S(2)}) async-start(), calls=%async_computation.18 | async-start | bytes 2654208 | tf_op jit(solution)/shard_map/reduce_scatter | solution.py:246
  269.7 156.8 %copy-start = (bf16[256,768]{1,0:T(8,128)(2,1)S(1)}, bf16[256,768]{1,0:T(8,128)(2,1)}, u32[]{:S(2)}) copy-start(bf16[256,768]{1,0:T(8,128)(2,1)} %param.15) | copy-start | bytes 1179652
  269.7 158.7 %copy-start.6 = (f32[256,768]{1,0:T(8,128)S(1)}, f32[256,768]{1,0:T(8,128)}, u32[]{:S(2)}) copy-start(f32[256,768]{1,0:T(8,128)} %param.17) | copy-start | bytes 2359300
  473.2 153.9 %copy-start.24 = (f32[24]{0:T(128)}, f32[24]{0:T(128)S(1)}, u32[]{:S(2)}) copy-start(f32[24]{0:T(128)S(1)} %dynamic-slice.6) | copy-start | bytes 292
  (6 other events, 13.0 us)
Sparse Core Ops, SparseCore 0:
  57.6 36.8 all-gather.7
  96.6 35.8 all-gather.15
  134.4 22.7 all-gather.11
  158.7 37.0 all-gather.9
  197.5 22.7 all-gather.13
  228.8 33.5 reduce-scatter.27
  266.1 34.9 reduce-scatter.25
  303.4 60.3 reduce-scatter.15
  366.2 60.3 reduce-scatter.17
  428.7 61.1 reduce-scatter.13
  493.9 40.1 reduce-scatter.19
  537.9 42.3 reduce-scatter.21
  584.2 42.3 reduce-scatter.23
where the time goes:
time: 640 us; the launch traced here: 634 us
  waiting for transfers between devices  347 us (54%)
  blocking collectives  136 us (21%)
  matrix products  86.3 us (13%)
  local copies, waits for them, and re-layouts  28.8 us (4%)
  other arithmetic  19.6 us (3%)
  between operations  15.4 us (2%)
    unnamed x3, blocking collectives  98.7 us
    reduce_scatter x1, waiting for transfers between devices, on_device(): lax.psum_scatter(second_part, 'tensor', scatter_dimension=0, tiled=True)  62.7 us
    reduce_scatter x1, waiting for transfers between devices, on_device(): lax.psum_scatter(first_part, 'tensor', scatter_dimension=0, tiled=True)  61.1 us
    reduce_scatter x1, waiting for transfers between devices, on_device(): lax.psum_scatter(grad_down, 'dp', scatter_dimension=1, tiled=True)  46.3 us
    reduce_scatter x1, waiting for transfers between devices, on_device(): lax.psum_scatter(grad_up, 'dp', scatter_dimension=0, tiled=True)  46.1 us
    reduce_scatter x1, waiting for transfers between devices, on_device(): lax.psum_scatter(grad_qkv, 'dp', scatter_dimension=0, tiled=True)  42.1 us
    all_gather x1, waiting for transfers between devices, on_device(): lax.all_gather(second_local, 'tensor', axis=0, tiled=True)  24.1 us
    all_gather x1, waiting for transfers between devices, on_device(): lax.all_gather(down_weight, 'dp', axis=1, tiled=True)  19.1 us
  transfers between devices with their start and end apart: 13, of which 10 were waited for; matrix products, arithmetic and copies ran while one was open for 18% of the time, Pallas kernels for 0%

commit v1 on v0

--- a/solution.py
+++ b/solution.py
@@ -153,9 +153,18 @@
     normed, inverse = normalize(wide_rows)
     first_local = (normed * gain_one + shift_one).astype(jnp.bfloat16)
     second_local = (normed * gain_two + shift_two).astype(jnp.bfloat16)
+
+    def name_ratios(target):
+        return jnp.concatenate(
+            lax.all_to_all(
+                jnp.stack(tuple((target for _ in range(lax.axis_size("tensor"))))), "tensor", 0, 0
+            ),
+            0,
+        )
+
     first, second = (
         lax.all_gather(first_local, "tensor", axis=0, tiled=True),
-        lax.all_gather(second_local, "tensor", axis=0, tiled=True),
+        name_ratios(second_local),
     )
     mixed = jnp.dot(first, qkv_full, preferred_element_type=jnp.float32) + qkv_shift.reshape(
         -1

time: 640 us -> 631 us (0.986)
  waiting for transfers between devices: 347 us -> 326 us
    all_gather x1 -> x0, waiting for transfers between devices: 24.1 us -> none  [on_device(): lax.all_gather(second_local, 'tensor', axis=0, tiled=True)]
    all_gather x1, waiting for transfers between devices: 19.1 us -> 0.01 us  [on_device(): lax.all_gather(down_weight, 'dp', axis=1, tiled=True)]
    all_gather x1, waiting for transfers between devices: 0.02 us -> 17 us  [on_device(): lax.all_gather(first_local, 'tensor', axis=0, tiled=True)]
    all_gather x1, waiting for transfers between devices: 18.3 us -> 24.7 us  [on_device(): lax.all_gather(cotangent.astype(jnp.bfloat16), 'tensor', axis=0, tiled=True)]
    unnamed x15 -> x14, waiting for transfers between devices: 13.1 us -> 11.6 us
    unnamed x76 -> x96, local copies, waits for them, and re-layouts: 17.1 us -> 17.2 us
  transfers between devices with their start and end apart: 13 -> 13, of which waited for: 10 -> 9; matrix products, arithmetic and copies ran while one was open for 18% -> 20% of each run, Pallas kernels for 0% -> 0%
where the time goes in v1:
time: 631 us; the launch traced here: 625 us
  waiting for transfers between devices  326 us (52%)
  blocking collectives  136 us (22%)
  matrix products  86.7 us (14%)
  local copies, waits for them, and re-layouts  31.5 us (5%)
  other arithmetic  24.3 us (4%)
  between operations  15.7 us (2%)
    unnamed x3, blocking collectives  98.6 us
    reduce_scatter x1, waiting for transfers between devices, on_device(): lax.psum_scatter(second_part, 'tensor', scatter_dimension=0, tiled=True)  62.6 us
    reduce_scatter x1, waiting for transfers between devices, on_device(): lax.psum_scatter(first_part, 'tensor', scatter_dimension=0, tiled=True)  61.1 us
    reduce_scatter x1, waiting for transfers between devices, on_device(): lax.psum_scatter(grad_up, 'dp', scatter_dimension=0, tiled=True)  46.3 us
    reduce_scatter x1, waiting for transfers between devices, on_device(): lax.psum_scatter(grad_down, 'dp', scatter_dimension=1, tiled=True)  46.2 us
    reduce_scatter x1, waiting for transfers between devices, on_device(): lax.psum_scatter(grad_qkv, 'dp', scatter_dimension=0, tiled=True)  41.9 us
    all_gather x1, waiting for transfers between devices, on_device(): lax.all_gather(cotangent.astype(jnp.bfloat16), 'tensor', axis=0, tiled=True)  24.7 us
    unnamed x96, local copies, waits for them, and re-layouts  17.2 us
  transfers between devices with their start and end apart: 13, of which 9 were waited for; matrix products, arithmetic and copies ran while one was open for 20% of the time, Pallas kernels for 0%

profile of v1, /device:TPU:0, one launch (start us, length us, event | category | flops | bytes accessed | tf_op | source)
XLA Modules:
  0.0 625.2 jit_solution(15156456520382054339)
XLA Ops:
  13.0 42.2 %all-reduce.13 = (f32[768]{0:T(1024)S(1)}, f32[768]{0:T(1024)S(1)}, f32[768]{0:T(1024)S(1)}, f32[768]{0:T(1024)S(1)}) all-reduce(f32[768]{0:T(1024)S(1)} %dynamic-update-slice.3, f32[768]{0:T(1024)S(1)} %dynamic-update-slice.2, f32[768]{0:T(1024)S(1)} %dynamic-update-slice.1, ...), channel_id=1, replica_groups=mesh['dp'=8,'tensor'=4] {'dp','tensor'}, use_global_device_ids=true, to_apply=%add.3 | all-reduce | flops 3072 | bytes 24576
  61.3 4.5 all-to-all-start
  66.5 11.6 %all_gather.49 = bf16[768,576]{1,0:T(8,128)(2,1)S(1)} all-gather(bf16[96,576]{1,0:T(8,128)(2,1)S(1)} %copy-done.24), channel_id=1, replica_groups=mesh['dp'=8,'tensor'=4] {'dp'}, dimensions={0}, use_global_device_ids=true | all-gather | bytes 995328 | tf_op jit(solution)/shard_map/all_gather | solution.py:139
  78.1 8.1 %all-gather = bf16[8,24,3]{1,2,0:T(4,128)(2,1)S(1)} all-gather(bf16[1,24,3]{1,2,0:T(4,128)(2,1)S(1)} %bitcast.92), channel_id=1, replica_groups=mesh['dp'=8,'tensor'=4] {'dp'}, dimensions={0}, use_global_device_ids=true | all-gather | bytes 1296 | tf_op jit(solution)/shard_map/all_gather | solution.py:145
  87.2 9.4 %all_gather.51 = bf16[192,768]{0,1:T(8,128)(2,1)S(1)} all-gather(bf16[192,96]{0,1:T(8,128)(2,1)S(1)} %copy.86), channel_id=1, replica_groups=mesh['dp'=8,'tensor'=4] {'dp'}, dimensions={1}, use_global_device_ids=true | all-gather | bytes 331776 | tf_op jit(solution)/shard_map/all_gather | solution.py:143
  96.7 8.1 %all-gather.1 = bf16[8,32,3]{1,2,0:T(4,128)(2,1)S(1)} all-gather(bf16[1,32,3]{1,2,0:T(4,128)(2,1)S(1)} %bitcast.93), channel_id=1, replica_groups=mesh['dp'=8,'tensor'=4] {'dp'}, dimensions={0}, use_global_device_ids=true | all-gather | bytes 1728 | tf_op jit(solution)/shard_map/all_gather | solution.py:146
  106.7 17.0 %all-gather.7.cloned.1.call-done = bf16[1024,768]{1,0:T(8,128)(2,1)} async-done(((bf16[256,768]{1,0:T(8,128)(2,1)}), bf16[1024,768]{1,0:T(8,128)(2,1)}) %all-gather.7.cloned.1.call-update) | async-done | bytes 1572880 | tf_op jit(solution)/shard_map/all_gather | solution.py:166
  123.7 4.0 convolution_add_fusion.1
  127.7 3.8 reshape.180
  136.4 24.7 %all-gather.13.cloned.1.call-done = bf16[1024,768]{1,0:T(8,128)(2,1)} async-done(((bf16[256,768]{1,0:T(8,128)(2,1)}), bf16[1024,768]{1,0:T(8,128)(2,1)}) %all-gather.13.cloned.1.call-update) | async-done | bytes 1572880 | tf_op jit(solution)/shard_map/all_gather | solution.py:195
  169.8 3.7 fusion.66
  173.5 12.7 %fusion.27 = f32[2,512,3,64]{1,3,2,0:T(8,128)S(1)} fusion(f32[2,3,512,512]{2,3,1,0:T(8,128)} %fusion.66, bf16[2,512,3,48]{1,3,2,0:T(8,128)(2,1)S(1)} %copy-done.21, bf16[2,512,3,16]{1,3,2,0:T(8,128)(2,1)S(1)} %copy-done.28, f32[2,3,512,512]{2,3,1,0:T(8,128)} %copy-done.1, f32[2,3,512]{2,1,0:T(4,128)S(1)} %log_add_fusion, pred[2,512,512]{1,2,0:T(8,128)(4,1)S(1)} %copy-done.8), kind=kOutput, calls=%fused_computation.31 | convolution fusion | flops 219418112 | bytes 14299136 | tf_op jit(solution)/shard_map/bhqk,bkhd->bqhd/dot_general | solution.py:89
  187.1 12.8 %fusion.30 = f32[2,512,3,64]{1,3,2,0:T(8,128)S(1)} fusion(f32[2,3,512,512]{2,3,1,0:T(8,128)} %fusion.66, bf16[2,512,3,48]{1,3,2,0:T(8,128)(2,1)S(1)} %copy-done.23, bf16[2,512,3,16]{1,3,2,0:T(8,128)(2,1)S(1)} %copy-done.26, f32[2,3,512,512]{2,3,1,0:T(8,128)} %copy-done.1, f32[2,3,512]{2,1,0:T(4,128)S(1)} %log_add_fusion, pred[2,512,512]{1,2,0:T(8,128)(4,1)S(1)} %copy-done.8), kind=kOutput, calls=%fused_computation.32 | convolution fusion | flops 219418112 | bytes 14299136 | tf_op jit(solution)/shard_map/bhqk,bqhd->bkhd/dot_general | solution.py:92
  200.9 4.5 fusion.36
  207.1 5.5 multiply_convert_fusion.1
  212.6 5.6 fusion.90
  226.6 4.8 fusion.24
  234.3 3.2 fusion.92
  237.6 4.8 fusion.62
  242.7 3.2 fusion.91
  248.3 4.5 fusion.93
  252.9 4.7 fusion.60
  257.6 4.3 fusion.94
  267.1 12.8 %all-reduce.10 = f32[3,192]{1,0:T(4,128)S(1)} all-reduce(f32[3,192]{1,0:T(4,128)S(1)} %reshape.184), channel_id=10, replica_groups=mesh['dp'=8,'tensor'=4] {'dp'}, use_global_device_ids=true, to_apply=%region_20.21.clone | all-reduce | flops 576 | bytes 4608
  281.9 10.3 %reduce-scatter.26.cloned.1.call-done = f32[96,192]{1,0:T(8,128)} async-done(((f32[768,192]{1,0:T(8,128)}), f32[96,192]{1,0:T(8,128)}) %reduce-scatter.26.cloned.1.call-update) | async-done | bytes 73744
  293.8 61.1 %reduce-scatter.16.cloned.1.call-done = f32[256,768]{1,0:T(8,128)} async-done(((f32[1024,768]{1,0:T(8,128)}), f32[256,768]{1,0:T(8,128)}) %reduce-scatter.16.cloned.1.call-update) | async-done | bytes 786448 | tf_op jit(solution)/shard_map/reduce_scatter | solution.py:224
  354.9 62.6 %reduce-scatter.18.cloned.1.call-done = f32[256,768]{1,0:T(8,128)} async-done(((f32[1024,768]{1,0:T(8,128)}), f32[256,768]{1,0:T(8,128)}) %reduce-scatter.18.cloned.1.call-update) | async-done | bytes 786448 | tf_op jit(solution)/shard_map/reduce_scatter | solution.py:225
  420.7 43.6 %all-reduce.12 = (f32[768]{0:T(1024)S(1)}, f32[768]{0:T(1024)S(1)}, f32[768]{0:T(1024)S(1)}, f32[768]{0:T(1024)S(1)}, f32[768]{0:T(1024)S(1)}, /*index=5*/f32[768]{0:T(1024)S(1)}, f32[768]{0:T(1024)S(1)}) all-reduce(f32[768]{0:T(1024)S(1)} %dynamic-update-slice.5, ...), channel_id=1, replica_groups=mesh['dp'=8,'tensor'=4] {'dp','tensor'}, use_global_device_ids=true, to_apply=%add.5 | all-reduce | flops 5376 | bytes 43008
  466.7 14.4 %reduce-scatter.14.cloned.1.call-done = f32[256,768]{1,0:T(8,128)} async-done(((f32[1024,768]{1,0:T(8,128)}), f32[256,768]{1,0:T(8,128)}) %reduce-scatter.14.cloned.1.call-update) | async-done | bytes 786448 | tf_op jit(solution)/shard_map/reduce_scatter | solution.py:185
  483.2 41.9 %reduce-scatter.20.cloned.1.call-done = f32[96,576]{1,0:T(8,128)} async-done(((f32[768,576]{1,0:T(8,128)}), f32[96,576]{1,0:T(8,128)}) %reduce-scatter.20.cloned.1.call-update) | async-done | bytes 221200 | tf_op jit(solution)/shard_map/reduce_scatter | solution.py:250
  525.1 46.3 %reduce-scatter.22.cloned.1.call-done = f32[96,768]{1,0:T(8,128)} async-done(((f32[768,768]{1,0:T(8,128)}), f32[96,768]{1,0:T(8,128)}) %reduce-scatter.22.cloned.1.call-update) | async-done | bytes 294928 | tf_op jit(solution)/shard_map/reduce_scatter | solution.py:251
  571.4 46.2 %reduce-scatter.24.cloned.1.call-done = f32[768,96]{0,1:T(8,128)} async-done(((f32[768,768]{0,1:T(8,128)}), f32[768,96]{0,1:T(8,128)}) %reduce-scatter.24.cloned.1.call-update) | async-done | bytes 294928 | tf_op jit(solution)/shard_map/reduce_scatter | solution.py:255
  (178 shorter events, 62.6 us)
Async XLA Ops:
  7.2 116.5 %all-gather.7.cloned.1.call-start = ((), (), s32[]{:S(2)}) async-start(), calls=%async_computation.9 | async-start | bytes 1966080 | tf_op jit(solution)/shard_map/all_gather | solution.py:166
  57.2 103.8 %all-gather.13.cloned.1.call-start = ((), (), s32[]{:S(2)}) async-start(), calls=%async_computation.13 | async-start | bytes 1966080 | tf_op jit(solution)/shard_map/all_gather | solution.py:195
  59.2 7.3 %copy-start.24 = (bf16[96,576]{1,0:T(8,128)(2,1)S(1)}, bf16[96,576]{1,0:T(8,128)(2,1)}, u32[]{:S(2)}) copy-start(bf16[96,576]{1,0:T(8,128)(2,1)} %param.22) | copy-start | bytes 331780
  59.3 147.8 %all-gather.9.cloned.1.call-start = ((), (), s32[]{:S(2)}) async-start(), calls=%async_computation.10 | async-start | bytes 1327104 | tf_op jit(solution)/shard_map/all_gather | solution.py:140
  60.0 18.1 %copy-start.32 = (bf16[3,24]{1,0:T(4,128)(2,1)S(1)}, bf16[3,24]{1,0:T(4,128)(2,1)}, u32[]{:S(2)}) copy-start(bf16[3,24]{1,0:T(4,128)(2,1)} %param.23) | copy-start | bytes 436
  60.0 27.1 %copy-start.29 = (bf16[192,96]{1,0:T(8,128)(2,1)S(1)}, bf16[192,96]{1,0:T(8,128)(2,1)}, u32[]{:S(2)}) copy-start(bf16[192,96]{1,0:T(8,128)(2,1)} %param.24) | copy-start | bytes 110596
  61.3 35.4 %copy-start.33 = (bf16[3,32]{1,0:T(4,128)(2,1)S(1)}, bf16[3,32]{1,0:T(4,128)(2,1)}, u32[]{:S(2)}) copy-start(bf16[3,32]{1,0:T(4,128)(2,1)} %param.27) | copy-start | bytes 580
  61.3 44.2 %copy-start.30 = (s32[2,512]{1,0:T(2,128)S(1)}, s32[2,512]{1,0:T(2,128)}, u32[]{:S(2)}) copy-start(s32[2,512]{1,0:T(2,128)} %param.16) | copy-start | bytes 12292
  61.3 145.8 %all-to-all-start = ((bf16[4,256,768]{2,1,0:T(8,128)(2,1)}), bf16[4,256,768]{2,1,0:T(8,128)(2,1)}, u32[]{:S(2)}, u32[]{:S(2)}) async-start(bf16[4,256,768]{2,1,0:T(8,128)(2,1)} %stack.19), calls=%async_computation | async-start | bytes 3145728 | tf_op jit(solution)/shard_map/all_to_all | solution.py:159
  65.8 146.8 %all-gather.11.cloned.1.call-start = ((), (), s32[]{:S(2)}) async-start(), calls=%async_computation.11 | async-start | bytes 1327104 | tf_op jit(solution)/shard_map/all_gather | solution.py:144
  66.3 214.2 %reduce-scatter.28.cloned.1.call-start = ((), (), s32[]{:S(2)}) async-start(), calls=%async_computation.20 | async-start | bytes 147456
  78.1 45.6 %copy-start.13 = (bf16[768,576]{1,0:T(8,128)(2,1)}, bf16[768,576]{1,0:T(8,128)(2,1)S(1)}, u32[]{:S(2)}) copy-start(bf16[768,576]{1,0:T(8,128)(2,1)S(1)} %all_gather.49) | copy-start | bytes 2654212
  136.3 27.1 %copy-start.15 = (f32[2,512,3,8]{1,3,2,0:T(8,128)S(1)}, f32[2,512,3,8]{1,3,2,0:T(8,128)}, u32[]{:S(2)}) copy-start(f32[2,512,3,8]{1,3,2,0:T(8,128)} %get-tuple-element.42) | copy-start | bytes 294916
  136.3 27.1 %copy-start.16 = (f32[2,512,3,8]{1,3,2,0:T(8,128)S(1)}, f32[2,512,3,8]{1,3,2,0:T(8,128)}, u32[]{:S(2)}) copy-start(f32[2,512,3,8]{1,3,2,0:T(8,128)} %get-tuple-element.43) | copy-start | bytes 294916
  136.3 27.1 %copy-start.17 = (f32[2,512,3,8]{1,3,2,0:T(8,128)S(1)}, f32[2,512,3,8]{1,3,2,0:T(8,128)}, u32[]{:S(2)}) copy-start(f32[2,512,3,8]{1,3,2,0:T(8,128)} %get-tuple-element.40) | copy-start | bytes 294916
  136.3 27.1 %copy-start.18 = (f32[2,512,3,8]{1,3,2,0:T(8,128)S(1)}, f32[2,512,3,8]{1,3,2,0:T(8,128)}, u32[]{:S(2)}) copy-start(f32[2,512,3,8]{1,3,2,0:T(8,128)} %get-tuple-element.41) | copy-start | bytes 294916
  136.3 28.3 %copy-start.20 = (bf16[2,512,3,48]{1,3,2,0:T(8,128)(2,1)S(1)}, bf16[2,512,3,48]{1,3,2,0:T(8,128)(2,1)}, u32[]{:S(2)}) copy-start(bf16[2,512,3,48]{1,3,2,0:T(8,128)(2,1)} %slice.122) | copy-start | bytes 884740
  136.4 28.3 %copy-start.22 = (bf16[2,512,3,48]{1,3,2,0:T(8,128)(2,1)S(1)}, bf16[2,512,3,48]{1,3,2,0:T(8,128)(2,1)}, u32[]{:S(2)}) copy-start(bf16[2,512,3,48]{1,3,2,0:T(8,128)(2,1)} %slice.123) | copy-start | bytes 884740
  169.8 31.1 %copy-start.31 = (f32[2,3,512]{2,1,0:T(4,128)}, f32[2,3,512]{2,1,0:T(4,128)S(1)}, u32[]{:S(2)}) copy-start(f32[2,3,512]{2,1,0:T(4,128)S(1)} %log_add_fusion) | copy-start | bytes 36868
  173.5 13.5 %copy-start.23 = (bf16[2,512,3,48]{1,3,2,0:T(8,128)(2,1)S(1)}, bf16[2,512,3,48]{1,3,2,0:T(8,128)(2,1)}, u32[]{:S(2)}) copy-start(bf16[2,512,3,48]{1,3,2,0:T(8,128)(2,1)} %slice.123) | copy-start | bytes 884740
  173.5 13.5 %copy-start.26 = (bf16[2,512,3,16]{1,3,2,0:T(8,128)(2,1)S(1)}, bf16[2,512,3,16]{1,3,2,0:T(8,128)(2,1)}, u32[]{:S(2)}) copy-start(bf16[2,512,3,16]{1,3,2,0:T(8,128)(2,1)} %copy-done.25) | copy-start | bytes 294916
  205.9 17.9 %copy-start.3 = (bf16[24,8,2,512]{3,1,2,0:T(8,128)(2,1)}, bf16[24,8,2,512]{3,1,2,0:T(8,128)(2,1)S(1)}, u32[]{:S(2)}) copy-start(bf16[24,8,2,512]{3,1,2,0:T(8,128)(2,1)S(1)} %copy.108) | copy-start | bytes 1179652
  220.9 71.3 %reduce-scatter.26.cloned.1.call-start = ((), (), s32[]{:S(2)}) async-start(), calls=%async_computation.19 | async-start | bytes 884736
  226.6 128.3 %reduce-scatter.16.cloned.1.call-start = ((), (), s32[]{:S(2)}) async-start(), calls=%async_computation.14 | async-start | bytes 3932160 | tf_op jit(solution)/shard_map/reduce_scatter | solution.py:224
  237.5 180.0 %reduce-scatter.18.cloned.1.call-start = ((), (), s32[]{:S(2)}) async-start(), calls=%async_computation.15 | async-start | bytes 3932160 | tf_op jit(solution)/shard_map/reduce_scatter | solution.py:225
  242.4 238.7 %reduce-scatter.14.cloned.1.call-start = ((), (), s32[]{:S(2)}) async-start(), calls=%async_computation.12 | async-start | bytes 3932160 | tf_op jit(solution)/shard_map/reduce_scatter | solution.py:185
  248.2 276.9 %reduce-scatter.20.cloned.1.call-start = ((), (), s32[]{:S(2)}) async-start(), calls=%async_computation.16 | async-start | bytes 2211840 | tf_op jit(solution)/shard_map/reduce_scatter | solution.py:250
  252.8 318.6 %reduce-scatter.22.cloned.1.call-start = ((), (), s32[]{:S(2)}) async-start(), calls=%async_computation.17 | async-start | bytes 2654208 | tf_op jit(solution)/shard_map/reduce_scatter | solution.py:251
  257.6 360.0 %reduce-scatter.24.cloned.1.call-start = ((), (), s32[]{:S(2)}) async-start(), calls=%async_computation.18 | async-start | bytes 2654208 | tf_op jit(solution)/shard_map/reduce_scatter | solution.py:255
  261.9 155.6 %copy-start = (bf16[256,768]{1,0:T(8,128)(2,1)S(1)}, bf16[256,768]{1,0:T(8,128)(2,1)}, u32[]{:S(2)}) copy-start(bf16[256,768]{1,0:T(8,128)(2,1)} %param.15) | copy-start | bytes 1179652
  261.9 157.5 %copy-start.6 = (f32[256,768]{1,0:T(8,128)S(1)}, f32[256,768]{1,0:T(8,128)}, u32[]{:S(2)}) copy-start(f32[256,768]{1,0:T(8,128)} %param.17) | copy-start | bytes 2359300
  464.4 153.7 %copy-start.34 = (f32[24]{0:T(128)}, f32[24]{0:T(128)S(1)}, u32[]{:S(2)}) copy-start(f32[24]{0:T(128)S(1)} %dynamic-slice.6) | copy-start | bytes 292
  (16 other events, 53.4 us)
Sparse Core Ops, SparseCore 0:
  57.4 66.2 all-gather.6
  125.2 35.7 all-gather.12
  162.9 22.7 all-gather.8
  187.5 23.9 all-gather.10
  221.0 32.4 reduce-scatter.27
  257.1 35.0 reduce-scatter.25
  294.5 60.3 reduce-scatter.15
  357.2 60.3 reduce-scatter.17
  419.9 61.2 reduce-scatter.13
  485.0 40.1 reduce-scatter.19
  529.1 42.3 reduce-scatter.21
  575.2 42.3 reduce-scatter.23
